TPU v7x, 256 devices: a whole 4x4x8 slice. The times are simulated.
256 devices in a mesh: rows: 8 (over z_hi, x), lat: 32 (over y, z_lo, core).
Axes of the slice: x: 4, y: 4, z: 8 (z_hi: 2, z_lo: 4; z = z_hi * 4 + z_lo), core: 2. Of those that a mesh axis runs over, the one named last changes fastest.
Arguments:
- residual: bfloat16 [1024, 4608], P('rows', 'lat'), may hold values from -64 to 64
- enc_weight: bfloat16 [4608, 65536], P('rows', 'lat'), may hold values from -0.09375 to 0.09375
- dec_weight: bfloat16 [65536, 4608], P('lat', 'rows'), may hold values from -0.078125 to 0.078125
- enc_bias: float32 [65536], P('lat'), may hold values from -3 to 3
- dec_bias: float32 [4608], P('rows'), may hold values from -3 to 3
- active_blocks: int32 [8, 96], replicated, may hold values from 0 to 511, as said below
- active_counts: int32 [1024], P('rows'), may hold values from 1 to 96, as said below
Outputs:
- latents: bfloat16 [1024, 65536], P('rows', 'lat')
- recon: bfloat16 [1024, 4608], P('lat', 'rows')
Inputs may be any that keep to these rules, and one draw needn't show every extreme that they name: `active_blocks`: each row lists 96 different latent blocks; at most 6 of them lie among the 16 blocks of one index of lat, and exactly 6 for some index in every row. `active_counts`: in every row block some row uses all 96 entries and some row uses one.
All inputs are finite; a program needn't handle non-finite values.
Results may differ from a plain program's by a relative error of at most 0.0058.
Values may be sent and summed in bfloat16 or wider, within the bound.
No kernel may reach another device: no remote copies, remote signals or barrier semaphores. Data moves between devices by JAX's collectives and lax.ppermute only.
A program may use at most 128 MiB of HBM per device.

v0:
```python
import jax
import jax.numpy as jnp
from jax import lax
from jax.sharding import PartitionSpec as P

BLOCK = 128


def shards(residual, enc_weight, dec_weight, enc_bias, dec_bias, active_blocks, active_counts):
    own_rows = residual.shape[0]
    row_count = lax.axis_size("rows")
    tokens_all = own_rows * row_count
    residual_t = residual.T
    full_t = lax.all_gather(residual_t, "lat", axis=0, tiled=True)
    width = full_t.shape[0]
    gram_block = lax.dot_general(
        residual_t, full_t, (((1,), (1,)), ((), ())), preferred_element_type=jnp.float32
    )
    gram_block = lax.psum(gram_block, "rows")
    wide_own = residual_t.astype(jnp.float32)
    energy = lax.psum(jnp.sum(wide_own * wide_own), ("rows", "lat"))
    mean_sq = energy / (tokens_all * width)
    chat = (gram_block / (tokens_all * (mean_sq + 1e-05))).astype(jnp.bfloat16)
    term = lax.dot_general(
        chat, residual_t, (((0,), (0,)), ((), ())), preferred_element_type=jnp.float32
    )
    term = lax.psum(term, "lat")
    white_t = (1.5 * full_t.astype(jnp.float32) - 0.5 * term).astype(jnp.bfloat16)
    shard_width = enc_weight.shape[1]
    pre = lax.dot_general(
        white_t,
        lax.all_gather(enc_weight, "rows", axis=0, tiled=True),
        (((0,), (0,)), ((), ())),
        preferred_element_type=jnp.float32,
    )
    pre = pre + enc_bias
    shard_blocks = shard_width // BLOCK
    own_blocks = own_rows // BLOCK
    listed_count = active_blocks.shape[1]
    lat_index = lax.axis_index("lat")
    row_index = lax.axis_index("rows")
    global_ids = lat_index * shard_blocks + jnp.arange(shard_blocks, dtype=jnp.int32)
    matches = active_blocks[:, :, None] == global_ids[None, None, :]
    slots = jnp.arange(listed_count, dtype=jnp.int32)[None, :, None]
    listed = jnp.any(matches, axis=1)
    slot_rank = jnp.sum(jnp.where(matches, slots, 0), axis=1) + listed_count * (
        1 - listed.astype(jnp.int32)
    )
    own_rank = lax.dynamic_slice_in_dim(slot_rank, row_index * own_blocks, own_blocks, 0)
    live = own_rank[:, None, :] < active_counts.reshape(own_blocks, BLOCK)[:, :, None]
    shaped = jnp.maximum(pre, 0.0).reshape(own_blocks, BLOCK, shard_blocks, BLOCK) * live[
        :, :, :, None
    ].astype(jnp.float32)
    latents = shaped.reshape(own_rows, shard_width).astype(jnp.bfloat16)
    terms = jnp.dot(
        lax.all_gather(latents, "rows", axis=0, tiled=True),
        dec_weight,
        preferred_element_type=jnp.float32,
    )
    recon_part = lax.psum_scatter(terms, "lat", scatter_dimension=0, tiled=True)
    recon = (recon_part + dec_bias).astype(jnp.bfloat16)
    return (latents, recon)


def solution(mesh):
    in_specs = (
        P("rows", "lat"),
        P("rows", "lat"),
        P("lat", "rows"),
        P("lat"),
        P("rows"),
        P(),
        P("rows"),
    )
    out_specs = (P("rows", "lat"), P("lat", "rows"))
    return jax.shard_map(shards, mesh=mesh, in_specs=in_specs, out_specs=out_specs, check_vma=False)
```

profile of v0, /device:TPU:2, one launch (start us, length us, event | category | flops | bytes accessed | tf_op | source)
XLA Modules:
  0.0 1131.7 jit_solution(10821013051532588925)
XLA Ops:
  7.2 0.0 copy-start
  7.2 0.0 all-gather.4.cloned.1.call-start
  7.2 0.7 all-gather.4.cloned.1.call-update
  7.9 0.0 copy-start.2
  7.9 0.0 all-reduce.3.cloned.1.call-start
  8.0 63.8 %all-gather.4.cloned.1.call-done = bf16[4608,128]{1,0:T(8,128)(2,1)} async-done(((bf16[144,128]{1,0:T(8,128)(2,1)}), bf16[4608,128]{1,0:T(8,128)(2,1)}) %all-gather.4.cloned.1.call-update) | async-done | bytes 1179664 | tf_op jit(solution)/shard_map/all_gather | solution.py:14
  71.7 3.3 fusion.9
  75.0 0.0 all-reduce.3.cloned.1.call-update
  75.1 0.0 all-reduce.5.cloned.1.call-start
  75.1 0.0 copy-done.2
  75.1 0.6 multiply_reduce_fusion
  75.7 103.7 %psum.22 = f32[]{:T(128)} all-reduce(f32[]{:T(128)} %multiply_reduce_fusion), channel_id=1, replica_groups=mesh['rows'=8,'lat'=32] {'rows','lat'}, use_global_device_ids=true, to_apply=%region_2.0 | all-reduce | flops 1 | bytes 8 | tf_op jit(solution)/shard_map/psum | solution.py:21
  180.1 45.0 %all-reduce.3.cloned.1.call-done = f32[144,4608]{1,0:T(8,128)} async-done(((f32[144,4608]{1,0:T(8,128)}), f32[144,4608]{1,0:T(8,128)}) %all-reduce.3.cloned.1.call-update) | async-done | bytes 2654224 | tf_op jit(solution)/shard_map/psum | solution.py:19
  225.1 4.1 fusion.3
  229.2 0.0 copy-start.3
  229.2 0.0 all-reduce.5.cloned.1.call-update
  229.2 0.0 copy-start.1
  229.2 0.0 copy-start.4
  229.2 0.0 all-gather.6.cloned.1.call-start
  229.3 0.5 all-gather.6.cloned.1.call-update
  229.8 0.0 all-gather.8.cloned.1.call-start
  229.8 0.0 copy-done.3
  229.9 0.3 compare_reduce_fusion
  230.1 0.3 fusion.6
  230.5 0.7 compare_convert_fusion
  231.2 0.7 copy.9
  231.9 283.2 %all-reduce.5.cloned.1.call-done = f32[4608,128]{1,0:T(8,128)} async-done(((f32[4608,128]{1,0:T(8,128)}), f32[4608,128]{1,0:T(8,128)}) %all-reduce.5.cloned.1.call-update) | async-done | bytes 2359312 | tf_op jit(solution)/shard_map/psum | solution.py:27
  515.1 340.4 %all-gather.6.cloned.1.call-done = bf16[4608,2048]{1,0:T(8,128)(2,1)} async-done(((bf16[576,2048]{1,0:T(8,128)(2,1)}), bf16[4608,2048]{1,0:T(8,128)(2,1)}) %all-gather.6.cloned.1.call-update) | async-done | bytes 18874384 | tf_op jit(solution)/shard_map/all_gather | solution.py:32
  855.5 1.2 mul.45
  856.7 0.0 copy-done.1
  856.7 0.0 copy-done.4
  856.7 10.7 fusion.2
  867.4 0.0 all-gather.8.cloned.1.call-update
  867.4 0.0 reduce-scatter.2.cloned.1.call-start
  867.5 101.9 %all-gather.8.cloned.1.call-done = bf16[1024,2048]{1,0:T(8,128)(2,1)} async-done(((bf16[128,2048]{1,0:T(8,128)(2,1)}), bf16[1024,2048]{1,0:T(8,128)(2,1)}) %all-gather.8.cloned.1.call-update) | async-done | bytes 4194320 | tf_op jit(solution)/shard_map/all_gather | solution.py:56
  969.4 0.0 copy-done
  969.4 7.2 fusion.10
  976.5 0.0 copy-start.5
  976.5 0.0 reduce-scatter.2.cloned.1.call-update
  976.6 146.8 %reduce-scatter.2.cloned.1.call-done = f32[32,576]{1,0:T(8,128)} async-done(((f32[1024,576]{1,0:T(8,128)}), f32[32,576]{1,0:T(8,128)}) %reduce-scatter.2.cloned.1.call-update) | async-done | bytes 73744 | tf_op jit(solution)/shard_map/reduce_scatter | solution.py:60
  1123.3 0.0 copy-done.5
  1123.3 1.5 add_convert_fusion
  (3 shorter events, 0.0 us)
Async XLA Ops:
  7.2 962.2 %copy-start = (bf16[2048,576]{0,1:T(8,128)(2,1)S(1)}, bf16[2048,576]{0,1:T(8,128)(2,1)}, u32[]{:S(2)}) copy-start(bf16[2048,576]{0,1:T(8,128)(2,1)} %param.9) | copy-start | bytes 7077892
  7.2 64.5 %all-gather.4.cloned.1.call-start = ((), (), s32[]{:S(2)}) async-start(), calls=%async_computation.1 | async-start | bytes 1216512 | tf_op jit(solution)/shard_map/all_gather | solution.py:14
  7.9 67.2 %copy-start.2 = (bf16[128,144]{0,1:T(8,128)(2,1)S(1)}, bf16[128,144]{0,1:T(8,128)(2,1)}, u32[]{:S(2)}) copy-start(bf16[128,144]{0,1:T(8,128)(2,1)} %param.7) | copy-start | bytes 110596
  7.9 217.2 %all-reduce.3.cloned.1.call-start = ((), (), s32[]{:S(2)}) async-start(), calls=%async_computation.2 | async-start | bytes 5308416 | tf_op jit(solution)/shard_map/psum | solution.py:19
  75.1 440.1 %all-reduce.5.cloned.1.call-start = ((), (), s32[]{:S(2)}) async-start(), calls=%async_computation.3 | async-start | bytes 4718592 | tf_op jit(solution)/shard_map/psum | solution.py:27
  229.2 0.7 copy-start.3
  229.2 627.5 %copy-start.1 = (bf16[4608,128]{1,0:T(8,128)(2,1)S(1)}, bf16[4608,128]{1,0:T(8,128)(2,1)}, u32[]{:S(2)}) copy-start(bf16[4608,128]{1,0:T(8,128)(2,1)} %all-gather.4.cloned.1.call-done) | copy-start | bytes 3538948
  229.2 627.5 %copy-start.4 = (f32[2048]{0:T(1024)S(1)}, f32[2048]{0:T(1024)}, u32[]{:S(2)}) copy-start(f32[2048]{0:T(1024)} %param.10) | copy-start | bytes 24580
  229.2 626.3 %all-gather.6.cloned.1.call-start = ((), (), s32[]{:S(2)}) async-start(), calls=%async_computation.4 | async-start | bytes 21233664 | tf_op jit(solution)/shard_map/all_gather | solution.py:32
  229.8 739.6 %all-gather.8.cloned.1.call-start = ((), (), s32[]{:S(2)}) async-start(), calls=%async_computation.5 | async-start | bytes 4718592 | tf_op jit(solution)/shard_map/all_gather | solution.py:56
  867.4 255.9 %reduce-scatter.2.cloned.1.call-start = ((), (), s32[]{:S(2)}) async-start(), calls=%async_computation.6 | async-start | bytes 2703360 | tf_op jit(solution)/shard_map/reduce_scatter | solution.py:60
  976.5 146.8 %copy-start.5 = (f32[576]{0:T(1024)S(1)}, f32[576]{0:T(1024)}, u32[]{:S(2)}) copy-start(f32[576]{0:T(1024)} %param.11) | copy-start | bytes 6916
Sparse Core Ops, SparseCore 0:
  9.8 61.8 all-gather.3
  75.2 149.8 all-reduce.2
  229.3 285.7 all-reduce.4
  517.6 337.8 all-gather.5
  867.6 101.7 all-gather.7
  976.7 146.6 reduce-scatter.1
where the time goes:
time: 1130 us
  waiting for transfers between devices  982 us (87%)
  blocking collectives  104 us (9%)
  matrix products  25.3 us (2%)
  between operations  14.9 us (1%)
    all_gather x1, waiting for transfers between devices, shards(): lax.all_gather(enc_weight, 'rows', axis=0, tiled=True)  340 us
    psum x1, waiting for transfers between devices, shards(): term = lax.psum(term, 'lat')  283 us
    reduce_scatter x1, waiting for transfers between devices, shards(): recon_part = lax.psum_scatter(terms, 'lat', scatter_dimension=0, tiled=True)  147 us
    psum x1, blocking collectives, shards(): energy = lax.psum(jnp.sum(wide_own * wide_own), ('rows', 'lat'))  104 us
    all_gather x1, waiting for transfers between devices, shards(): lax.all_gather(latents, 'rows', axis=0, tiled=True)  102 us
    all_gather x1, waiting for transfers between devices, shards(): full_t = lax.all_gather(residual_t, 'lat', axis=0, tiled=True)  63.8 us
    psum x1, waiting for transfers between devices, shards(): gram_block = lax.psum(gram_block, 'rows')  45 us
  transfers between devices with their start and end apart: 6, of which 6 were waited for; matrix products, arithmetic and copies ran while one was open for 0% of the time, Pallas kernels for 0%

commit v1 on v0

--- a/solution.py
+++ b/solution.py
@@ -24,7 +24,7 @@
     term = lax.dot_general(
         chat, residual_t, (((0,), (0,)), ((), ())), preferred_element_type=jnp.float32
     )
-    term = lax.psum(term, "lat")
+    term = jnp.sum(lax.all_gather(term, "lat"), axis=0)
     white_t = (1.5 * full_t.astype(jnp.float32) - 0.5 * term).astype(jnp.bfloat16)
     shard_width = enc_weight.shape[1]
     pre = lax.dot_general(

time: 1130 us -> 1240 us (1.097)
  waiting for transfers between devices: 982 us -> 1070 us
  other arithmetic: 3.43 us -> 29.8 us
    all_gather x0 -> x1, waiting for transfers between devices: none -> 394 us  [shards(): term = jnp.sum(lax.all_gather(term, 'lat'), axis=0)]
    psum x1 -> x0, waiting for transfers between devices: 283 us -> none  [shards(): term = lax.psum(term, 'lat')]
    reduce_sum x0 -> x1, other arithmetic: none -> 27 us  [shards(): term = jnp.sum(lax.all_gather(term, 'lat'), axis=0)]
    all_gather x1, waiting for transfers between devices: 340 us -> 315 us  [shards(): lax.all_gather(enc_weight, 'rows', axis=0, tiled=True)]
  transfers between devices with their start and end apart: 6 -> 6, of which waited for: 6 -> 6; matrix products, arithmetic and copies ran while one was open for 0% -> 2% of each run, Pallas kernels for 0% -> 0%
where the time goes in v1:
time: 1240 us
  waiting for transfers between devices  1070 us (86%)
  blocking collectives  104 us (8%)
  other arithmetic  29.8 us (2%)
  matrix products  25.3 us (2%)
  between operations  14.8 us (1%)
    all_gather x1, waiting for transfers between devices, shards(): term = jnp.sum(lax.all_gather(term, 'lat'), axis=0)  394 us
    all_gather x1, waiting for transfers between devices, shards(): lax.all_gather(enc_weight, 'rows', axis=0, tiled=True)  315 us
    reduce_scatter x1, waiting for transfers between devices, shards(): recon_part = lax.psum_scatter(terms, 'lat', scatter_dimension=0, tiled=True)  146 us
    psum x1, blocking collectives, shards(): energy = lax.psum(jnp.sum(wide_own * wide_own), ('rows', 'lat'))  104 us
    all_gather x1, waiting for transfers between devices, shards(): lax.all_gather(latents, 'rows', axis=0, tiled=True)  102 us
    all_gather x1, waiting for transfers between devices, shards(): full_t = lax.all_gather(residual_t, 'lat', axis=0, tiled=True)  63.8 us
    psum x1, waiting for transfers between devices, shards(): gram_block = lax.psum(gram_block, 'rows')  45 us
    reduce_sum x1, other arithmetic, shards(): term = jnp.sum(lax.all_gather(term, 'lat'), axis=0)  27 us
  transfers between devices with their start and end apart: 6, of which 6 were waited for; matrix products, arithmetic and copies ran while one was open for 2% of the time, Pallas kernels for 0%

profile of v1, /device:TPU:2, one launch (start us, length us, event | category | flops | bytes accessed | tf_op | source)
XLA Modules:
  0.0 1243.2 jit_solution(15043988740901542591)
XLA Ops:
  7.2 0.0 copy-start
  7.2 0.0 all-gather.6.cloned.1.call-start
  7.2 0.7 all-gather.6.cloned.1.call-update
  7.9 0.0 copy-start.2
  7.9 0.0 all-reduce.2.cloned.1.call-start
  8.0 63.8 %all-gather.6.cloned.1.call-done = bf16[4608,128]{1,0:T(8,128)(2,1)} async-done(((bf16[144,128]{1,0:T(8,128)(2,1)}), bf16[4608,128]{1,0:T(8,128)(2,1)}) %all-gather.6.cloned.1.call-update) | async-done | bytes 1179664 | tf_op jit(solution)/shard_map/all_gather | solution.py:14
  71.7 3.3 fusion.9
  75.0 0.0 all-reduce.2.cloned.1.call-update
  75.1 0.0 all-gather.12.cloned.1.call-start
  75.1 0.0 copy-done.2
  75.1 0.6 multiply_reduce_fusion
  75.7 104.4 %psum.15 = f32[]{:T(128)} all-reduce(f32[]{:T(128)} %multiply_reduce_fusion), channel_id=1, replica_groups=mesh['rows'=8,'lat'=32] {'rows','lat'}, use_global_device_ids=true, to_apply=%region_2.0 | all-reduce | flops 1 | bytes 8 | tf_op jit(solution)/shard_map/psum | solution.py:21
  180.8 45.0 %all-reduce.2.cloned.1.call-done = f32[144,4608]{1,0:T(8,128)} async-done(((f32[144,4608]{1,0:T(8,128)}), f32[144,4608]{1,0:T(8,128)}) %all-reduce.2.cloned.1.call-update) | async-done | bytes 2654224 | tf_op jit(solution)/shard_map/psum | solution.py:19
  225.7 4.0 fusion.3
  229.8 0.0 copy-start.3
  229.8 0.0 copy-start.6
  229.8 0.0 all-gather.12.cloned.1.call-update
  229.8 0.0 all-gather.8.cloned.1.call-start
  229.9 0.5 all-gather.8.cloned.1.call-update
  230.4 0.0 all-gather.10.cloned.1.call-start
  230.5 0.0 copy-done.3
  230.5 0.3 compare_reduce_fusion
  230.8 0.3 fusion.6
  231.1 0.0 copy-done.6
  231.1 0.1 compare_convert_fusion
  231.2 0.7 copy.9
  231.9 393.8 %all-gather.12.cloned.1.call-done = f32[147456,128]{1,0:T(8,128)} async-done(((f32[4608,128]{1,0:T(8,128)}), f32[147456,128]{1,0:T(8,128)}) %all-gather.12.cloned.1.call-update) | async-done | bytes 75497488 | tf_op jit(solution)/shard_map/all_gather | solution.py:27
  625.7 0.0 copy-start.1
  625.7 0.0 copy-start.4
  625.7 27.0 %reduce_sum.28 = f32[4608,128]{1,0:T(8,128)} reduce(f32[32,4608,128]{2,1,0:T(8,128)} %bitcast.1, f32[]{:T(128)} %constant.4.clone.1), dimensions={0}, to_apply=%region_3.0 | reduce | flops 18284544 | bytes 77856768 | tf_op jit(solution)/shard_map/reduce_sum | solution.py:27
  652.7 315.1 %all-gather.8.cloned.1.call-done = bf16[4608,2048]{1,0:T(8,128)(2,1)} async-done(((bf16[576,2048]{1,0:T(8,128)(2,1)}), bf16[4608,2048]{1,0:T(8,128)(2,1)}) %all-gather.8.cloned.1.call-update) | async-done | bytes 18874384 | tf_op jit(solution)/shard_map/all_gather | solution.py:32
  967.8 1.2 mul.45
  969.0 0.0 copy-done.1
  969.0 0.0 copy-done.4
  969.0 10.7 fusion.2
  979.7 0.0 all-gather.10.cloned.1.call-update
  979.7 0.0 reduce-scatter.2.cloned.1.call-start
  979.8 101.9 %all-gather.10.cloned.1.call-done = bf16[1024,2048]{1,0:T(8,128)(2,1)} async-done(((bf16[128,2048]{1,0:T(8,128)(2,1)}), bf16[1024,2048]{1,0:T(8,128)(2,1)}) %all-gather.10.cloned.1.call-update) | async-done | bytes 4194320 | tf_op jit(solution)/shard_map/all_gather | solution.py:56
  1081.7 0.0 copy-done
  1081.7 7.2 fusion.10
  1088.8 0.0 copy-start.5
  1088.8 0.0 reduce-scatter.2.cloned.1.call-update
  1088.9 146.0 %reduce-scatter.2.cloned.1.call-done = f32[32,576]{1,0:T(8,128)} async-done(((f32[1024,576]{1,0:T(8,128)}), f32[32,576]{1,0:T(8,128)}) %reduce-scatter.2.cloned.1.call-update) | async-done | bytes 73744 | tf_op jit(solution)/shard_map/reduce_scatter | solution.py:60
  1234.9 0.0 copy-done.5
  1234.9 1.5 add_convert_fusion
  (3 shorter events, 0.0 us)
Async XLA Ops:
  7.2 1074.5 %copy-start = (bf16[2048,576]{0,1:T(8,128)(2,1)S(1)}, bf16[2048,576]{0,1:T(8,128)(2,1)}, u32[]{:S(2)}) copy-start(bf16[2048,576]{0,1:T(8,128)(2,1)} %param.9) | copy-start | bytes 7077892
  7.2 64.5 %all-gather.6.cloned.1.call-start = ((), (), s32[]{:S(2)}) async-start(), calls=%async_computation.1 | async-start | bytes 1216512 | tf_op jit(solution)/shard_map/all_gather | solution.py:14
  7.9 67.2 %copy-start.2 = (bf16[128,144]{0,1:T(8,128)(2,1)S(1)}, bf16[128,144]{0,1:T(8,128)(2,1)}, u32[]{:S(2)}) copy-start(bf16[128,144]{0,1:T(8,128)(2,1)} %param.7) | copy-start | bytes 110596
  7.9 217.8 %all-reduce.2.cloned.1.call-start = ((), (), s32[]{:S(2)}) async-start(), calls=%async_computation.2 | async-start | bytes 5308416 | tf_op jit(solution)/shard_map/psum | solution.py:19
  75.1 550.7 %all-gather.12.cloned.1.call-start = ((), (), s32[]{:S(2)}) async-start(), calls=%async_computation.6 | async-start | bytes 77856768 | tf_op jit(solution)/shard_map/all_gather | solution.py:27
  229.8 0.7 copy-start.3
  229.8 1.3 copy-start.6
  229.8 738.0 %all-gather.8.cloned.1.call-start = ((), (), s32[]{:S(2)}) async-start(), calls=%async_computation.3 | async-start | bytes 21233664 | tf_op jit(solution)/shard_map/all_gather | solution.py:32
  230.4 851.3 %all-gather.10.cloned.1.call-start = ((), (), s32[]{:S(2)}) async-start(), calls=%async_computation.4 | async-start | bytes 4718592 | tf_op jit(solution)/shard_map/all_gather | solution.py:56
  625.7 343.3 %copy-start.1 = (bf16[4608,128]{1,0:T(8,128)(2,1)S(1)}, bf16[4608,128]{1,0:T(8,128)(2,1)}, u32[]{:S(2)}) copy-start(bf16[4608,128]{1,0:T(8,128)(2,1)} %all-gather.6.cloned.1.call-done) | copy-start | bytes 3538948
  625.7 343.3 %copy-start.4 = (f32[2048]{0:T(1024)S(1)}, f32[2048]{0:T(1024)}, u32[]{:S(2)}) copy-start(f32[2048]{0:T(1024)} %param.10) | copy-start | bytes 24580
  979.7 255.1 %reduce-scatter.2.cloned.1.call-start = ((), (), s32[]{:S(2)}) async-start(), calls=%async_computation.5 | async-start | bytes 2703360 | tf_op jit(solution)/shard_map/reduce_scatter | solution.py:60
  1088.8 146.0 %copy-start.5 = (f32[576]{0:T(1024)S(1)}, f32[576]{0:T(1024)}, u32[]{:S(2)}) copy-start(f32[576]{0:T(1024)} %param.11) | copy-start | bytes 6916
Sparse Core Ops, SparseCore 0:
  9.8 61.8 all-gather.5
  75.2 150.5 all-reduce.1
  229.9 395.7 all-gather.11
  628.2 339.5 all-gather.7
  979.9 101.7 all-gather.9
  1089.0 145.8 reduce-scatter.1

commit v2 on v0

--- a/solution.py
+++ b/solution.py
@@ -29,7 +29,9 @@
     shard_width = enc_weight.shape[1]
     pre = lax.dot_general(
         white_t,
-        lax.all_gather(enc_weight, "rows", axis=0, tiled=True),
+        jnp.concatenate(
+            lax.all_to_all(jnp.stack([enc_weight] * lax.axis_size("rows")), "rows", 0, 0), axis=0
+        ),
         (((0,), (0,)), ((), ())),
         preferred_element_type=jnp.float32,
     )

time: 1130 us -> 1200 us (1.062)
  waiting for transfers between devices: 982 us -> 1020 us
    all_gather x1, waiting for transfers between devices: 63.8 us -> 443 us  [shards(): full_t = lax.all_gather(residual_t, 'lat', axis=0, tiled=True)]
    all_gather x1 -> x0, waiting for transfers between devices: 340 us -> none  [shards(): lax.all_gather(enc_weight, 'rows', axis=0, tiled=True)]
  transfers between devices with their start and end apart: 6 -> 6, of which waited for: 6 -> 5; matrix products, arithmetic and copies ran while one was open for 0% -> 1% of each run, Pallas kernels for 0% -> 0%
where the time goes in v2:
time: 1200 us
  waiting for transfers between devices  1020 us (85%)
  blocking collectives  111 us (9%)
  matrix products  25.2 us (2%)
  between operations  14.5 us (1%)
    all_gather x1, waiting for transfers between devices, shards(): full_t = lax.all_gather(residual_t, 'lat', axis=0, tiled=True)  443 us
    psum x1, waiting for transfers between devices, shards(): term = lax.psum(term, 'lat')  284 us
    reduce_scatter x1, waiting for transfers between devices, shards(): recon_part = lax.psum_scatter(terms, 'lat', scatter_dimension=0, tiled=True)  147 us
    psum x1, blocking collectives, shards(): energy = lax.psum(jnp.sum(wide_own * wide_own), ('rows', 'lat'))  111 us
    all_gather x1, waiting for transfers between devices, shards(): lax.all_gather(latents, 'rows', axis=0, tiled=True)  105 us
    psum x1, waiting for transfers between devices, shards(): gram_block = lax.psum(gram_block, 'rows')  42.7 us
  transfers between devices with their start and end apart: 6, of which 5 were waited for; matrix products, arithmetic and copies ran while one was open for 1% of the time, Pallas kernels for 0%

profile of v2, /device:TPU:2, one launch (start us, length us, event | category | flops | bytes accessed | tf_op | source)
XLA Modules:
  0.0 1198.7 jit_solution(5023443767466472331)
XLA Ops:
  7.2 0.0 copy-start
  7.2 7.9 stack.2
  15.1 0.0 copy-start.2
  15.1 11.6 all-to-all-start
  26.7 0.0 all-gather.3.cloned.1.call-start
  26.7 0.7 all-gather.3.cloned.1.call-update
  27.4 0.0 all-reduce.3.cloned.1.call-start
  27.4 443.4 %all-gather.3.cloned.1.call-done = bf16[4608,128]{1,0:T(8,128)(2,1)} async-done(((bf16[144,128]{1,0:T(8,128)(2,1)}), bf16[4608,128]{1,0:T(8,128)(2,1)}) %all-gather.3.cloned.1.call-update) | async-done | bytes 1179664 | tf_op jit(solution)/shard_map/all_gather | solution.py:14
  470.8 0.0 copy-done.2
  470.8 3.3 fusion.9
  474.1 0.0 all-reduce.3.cloned.1.call-update
  474.1 0.0 all-reduce.5.cloned.1.call-start
  474.1 0.6 multiply_reduce_fusion
  474.8 110.9 %psum.22 = f32[]{:T(128)} all-reduce(f32[]{:T(128)} %multiply_reduce_fusion), channel_id=1, replica_groups=mesh['rows'=8,'lat'=32] {'rows','lat'}, use_global_device_ids=true, to_apply=%region_2.0 | all-reduce | flops 1 | bytes 8 | tf_op jit(solution)/shard_map/psum | solution.py:21
  586.3 42.7 %all-reduce.3.cloned.1.call-done = f32[144,4608]{1,0:T(8,128)} async-done(((f32[144,4608]{1,0:T(8,128)}), f32[144,4608]{1,0:T(8,128)}) %all-reduce.3.cloned.1.call-update) | async-done | bytes 2654224 | tf_op jit(solution)/shard_map/psum | solution.py:19
  629.0 4.1 fusion.3
  633.1 0.0 copy-start.3
  633.1 0.0 copy-start.1
  633.1 0.0 copy-start.4
  633.1 0.0 all-reduce.5.cloned.1.call-update
  633.1 0.0 all-gather.5.cloned.1.call-start
  633.2 0.6 copy-done.3
  633.8 0.3 compare_reduce_fusion
  634.0 0.3 fusion.6
  634.4 0.7 compare_convert_fusion
  635.1 0.7 copy.9
  635.8 284.3 %all-reduce.5.cloned.1.call-done = f32[4608,128]{1,0:T(8,128)} async-done(((f32[4608,128]{1,0:T(8,128)}), f32[4608,128]{1,0:T(8,128)}) %all-reduce.5.cloned.1.call-update) | async-done | bytes 2359312 | tf_op jit(solution)/shard_map/psum | solution.py:27
  920.1 0.0 all-to-all-done
  920.2 1.2 mul.45
  921.3 0.0 copy-done.1
  921.3 0.0 copy-done.4
  921.3 10.7 fusion.2
  932.1 0.0 all-gather.5.cloned.1.call-update
  932.1 0.0 reduce-scatter.2.cloned.1.call-start
  932.1 104.8 %all-gather.5.cloned.1.call-done = bf16[1024,2048]{1,0:T(8,128)(2,1)} async-done(((bf16[128,2048]{1,0:T(8,128)(2,1)}), bf16[1024,2048]{1,0:T(8,128)(2,1)}) %all-gather.5.cloned.1.call-update) | async-done | bytes 4194320 | tf_op jit(solution)/shard_map/all_gather | solution.py:58
  1036.9 0.0 copy-done
  1036.9 7.2 fusion.10
  1044.1 0.0 copy-start.5
  1044.1 0.0 reduce-scatter.2.cloned.1.call-update
  1044.1 146.6 %reduce-scatter.2.cloned.1.call-done = f32[32,576]{1,0:T(8,128)} async-done(((f32[1024,576]{1,0:T(8,128)}), f32[32,576]{1,0:T(8,128)}) %reduce-scatter.2.cloned.1.call-update) | async-done | bytes 73744 | tf_op jit(solution)/shard_map/reduce_scatter | solution.py:62
  1190.7 0.0 copy-done.5
  1190.7 1.5 add_convert_fusion
  (3 shorter events, 0.0 us)
Async XLA Ops:
  7.2 1029.8 %copy-start = (bf16[2048,576]{0,1:T(8,128)(2,1)S(1)}, bf16[2048,576]{0,1:T(8,128)(2,1)}, u32[]{:S(2)}) copy-start(bf16[2048,576]{0,1:T(8,128)(2,1)} %param.9) | copy-start | bytes 7077892
  15.1 455.7 %copy-start.2 = (bf16[128,144]{0,1:T(8,128)(2,1)S(1)}, bf16[128,144]{0,1:T(8,128)(2,1)}, u32[]{:S(2)}) copy-start(bf16[128,144]{0,1:T(8,128)(2,1)} %param.7) | copy-start | bytes 110596
  15.1 905.1 %all-to-all-start = ((bf16[8,576,2048]{2,1,0:T(8,128)(2,1)}), bf16[8,576,2048]{2,1,0:T(8,128)(2,1)}, u32[]{:S(2)}, u32[]{:S(2)}) async-start(bf16[8,576,2048]{2,1,0:T(8,128)(2,1)} %stack.2), calls=%async_computation | async-start | bytes 37748736 | tf_op jit(solution)/shard_map/all_to_all | solution.py:33
  26.7 444.1 %all-gather.3.cloned.1.call-start = ((), (), s32[]{:S(2)}) async-start(), calls=%async_computation.2 | async-start | bytes 1216512 | tf_op jit(solution)/shard_map/all_gather | solution.py:14
  27.4 601.6 %all-reduce.3.cloned.1.call-start = ((), (), s32[]{:S(2)}) async-start(), calls=%async_computation.3 | async-start | bytes 5308416 | tf_op jit(solution)/shard_map/psum | solution.py:19
  474.1 446.1 %all-reduce.5.cloned.1.call-start = ((), (), s32[]{:S(2)}) async-start(), calls=%async_computation.4 | async-start | bytes 4718592 | tf_op jit(solution)/shard_map/psum | solution.py:27
  633.1 0.7 copy-start.3
  633.1 288.3 %copy-start.1 = (bf16[4608,128]{1,0:T(8,128)(2,1)S(1)}, bf16[4608,128]{1,0:T(8,128)(2,1)}, u32[]{:S(2)}) copy-start(bf16[4608,128]{1,0:T(8,128)(2,1)} %all-gather.3.cloned.1.call-done) | copy-start | bytes 3538948
  633.1 288.3 %copy-start.4 = (f32[2048]{0:T(1024)S(1)}, f32[2048]{0:T(1024)}, u32[]{:S(2)}) copy-start(f32[2048]{0:T(1024)} %param.10) | copy-start | bytes 24580
  633.1 403.8 %all-gather.5.cloned.1.call-start = ((), (), s32[]{:S(2)}) async-start(), calls=%async_computation.5 | async-start | bytes 4718592 | tf_op jit(solution)/shard_map/all_gather | solution.py:58
  932.1 258.6 %reduce-scatter.2.cloned.1.call-start = ((), (), s32[]{:S(2)}) async-start(), calls=%async_computation.6 | async-start | bytes 2703360 | tf_op jit(solution)/shard_map/reduce_scatter | solution.py:62
  1044.1 146.6 %copy-start.5 = (f32[576]{0:T(1024)S(1)}, f32[576]{0:T(1024)}, u32[]{:S(2)}) copy-start(f32[576]{0:T(1024)} %param.11) | copy-start | bytes 6916
Sparse Core Ops, SparseCore 0:
  29.3 441.4 all-gather.2
  474.2 154.7 all-reduce.2
  633.2 286.8 all-reduce.4
  932.2 104.6 all-gather.4
  1044.2 146.4 reduce-scatter.1
